TPU v7x, 256 devices: a whole 4x4x8 slice. The times are simulated.
256 devices in a mesh: slab: 16 (over x, y), pencil: 16 (over z, core).
Axes of the slice: x: 4, y: 4, z: 8, core: 2. Of those that a mesh axis runs over, the one named last changes fastest.
Arguments:
- charges: bfloat16 [64, 131072], P(None, ('slab', 'pencil')), may hold values from -6 to 6
- cotangent: bfloat16 [64, 131072], P(None, ('slab', 'pencil')), may hold values from -6 to 6
- base_cell: int32 [3, 131072], P(None, ('slab', 'pencil')), may hold values from 0 to 63, as said below
- frac: float32 [3, 131072], P(None, ('slab', 'pencil')), may hold values from 0 to 1
- counts: int32 [256], P(('slab', 'pencil')), may hold values from 256 to 512, as said below
- filter_weights: float32 [32, 64], replicated, may hold values from -6 to 6
Outputs:
- potential: bfloat16 [64, 131072], P(None, ('slab', 'pencil'))
- charge_grad: bfloat16 [64, 131072], P(None, ('slab', 'pencil'))
- filter_grad: float32 [32, 64], replicated
Inputs may be any that keep to these rules, and one draw needn't show every extreme that they name: `base_cell`: slots d * 512 to (d + 1) * 512 - 1 belong to device d = slab index * (pencil axis size) + pencil index; their first cell index lies in the slab index's run of 4 cells and their second in the pencil index's run of 4 cells; the third is any cell. A device's live atoms are its first counts slots; some device's count is 512.
All inputs are finite; a program needn't handle non-finite values.
Results may differ from a plain program's by a relative error of at most 0.013.
Values may be sent and summed in bfloat16 or wider, within the bound.
A program may use at most 128 MiB of HBM per device.

v0:
```python
import jax
import jax.numpy as jnp
from jax import lax
from jax.sharding import PartitionSpec as P

N = 64
C = 64
NB = 32
ENV_SCALE = 40.0
ENV_WIDTH = 16.0


def passed_along(value, axis, steps):
    count = lax.axis_size(axis)
    pairs = [(source, (source + steps) % count) for source in range(count)]
    return lax.ppermute(value, axis, pairs)


def spline_weights(frac):
    remain = 1.0 - frac
    square = frac * frac
    cubed = square * frac
    weight_zero = remain * remain * remain / 6.0
    weight_one = (3.0 * cubed - 6.0 * square + 4.0) / 6.0
    weight_two = (-3.0 * cubed + 3.0 * square + 3.0 * frac + 1.0) / 6.0
    weight_three = cubed / 6.0
    return jnp.stack([weight_zero, weight_one, weight_two, weight_three], axis=1)


def stencil_local(base_cell, frac, live, x_first, y_first, span_y):
    weights = spline_weights(frac)
    offsets = jnp.arange(64, dtype=jnp.int32)
    along_x = jnp.repeat(weights[0], 16, axis=0)
    along_y = jnp.tile(jnp.repeat(weights[1], 4, axis=0), (4, 1))
    along_z = jnp.tile(weights[2], (16, 1))
    stencil = along_x * along_y * along_z * live[None, :]
    local_x = base_cell[0][None, :] - x_first + offsets[:, None] // 16
    local_y = base_cell[1][None, :] - y_first + offsets[:, None] // 4 % 4
    local_z = (base_cell[2][None, :] + offsets[:, None] % 4) % N
    cell_ids = (local_x * (span_y + 3) + local_y) * N + local_z
    return (cell_ids, stencil)


def frequencies(positions):
    return jnp.where(positions < N // 2, positions, positions - N).astype(jnp.float32)


def filter_shells(y_first, z_first, y_count, z_count):
    freq_x = frequencies(jnp.arange(N, dtype=jnp.int32))
    freq_y = frequencies(y_first + jnp.arange(y_count, dtype=jnp.int32))
    freq_z = frequencies(z_first + jnp.arange(z_count, dtype=jnp.int32))
    kappa_sq = (
        freq_x[:, None, None] * freq_x[:, None, None]
        + freq_y[None, :, None] * freq_y[None, :, None]
        + freq_z[None, None, :] * freq_z[None, None, :]
    )
    kappa = jnp.sqrt(kappa_sq)
    envelope = ENV_SCALE * ENV_WIDTH / (ENV_WIDTH + kappa_sq)
    spacing = N / (2.0 * NB)
    centers = (jnp.arange(NB, dtype=jnp.float32) + 0.5) * spacing
    shells = envelope[..., None] * jnp.exp(-jnp.square((kappa[..., None] - centers) / spacing))
    return shells.reshape(N * y_count * z_count, NB)


def dft_tables(length):
    indices = jnp.arange(length, dtype=jnp.int32)
    phases = indices[:, None] * indices[None, :] % length
    angles = phases.astype(jnp.float32) * (2.0 * jnp.pi / length)
    return (jnp.cos(angles), jnp.sin(angles))


def contract(operand, matrix, pattern):
    if operand.dtype == jnp.bfloat16:
        table_high = matrix.astype(jnp.bfloat16)
        table_low = (matrix - table_high.astype(jnp.float32)).astype(jnp.bfloat16)
        first = jnp.einsum(pattern, operand, table_high, preferred_element_type=jnp.float32)
        second = jnp.einsum(pattern, operand, table_low, preferred_element_type=jnp.float32)
        return first + second
    return jnp.einsum(pattern, operand, matrix, precision=lax.Precision.HIGHEST)


def transform(values, pattern, inverse, real_in, real_out):
    cosines, sines = dft_tables(N)
    direction = 1.0 if inverse else -1.0
    factor = 1.0 / N if inverse else 1.0
    if real_in:
        real_part = values
        new_real = contract(real_part, cosines, pattern)
        new_imag = direction * contract(real_part, sines, pattern)
    else:
        halfway = values.shape[-1] // 2
        real_part = values[..., :halfway]
        imag_part = values[..., halfway:]
        new_real = contract(real_part, cosines, pattern) - direction * contract(
            imag_part, sines, pattern
        )
        if real_out:
            return new_real * factor
        new_imag = contract(imag_part, cosines, pattern) + direction * contract(
            real_part, sines, pattern
        )
    return jnp.concatenate([new_real, new_imag], axis=-1) * factor


def spread(values, cell_ids, stencil, span_x, span_y, blocks_run):
    channels = values.shape[1]
    total_cells = (span_x + 3) * (span_y + 3) * N

    def add_block(number, totals):
        block_vals = values.astype(jnp.float32)
        products = stencil[:, :, None] * block_vals[None, :, :]
        return totals.at[cell_ids.reshape(-1)].add(products.reshape(-1, channels))

    totals = lax.fori_loop(
        0, blocks_run, add_block, jnp.zeros((total_cells, channels), jnp.float32)
    )
    totals = totals.reshape(span_x + 3, span_y + 3, N, channels)
    rim_planes = passed_along(totals[span_x:].astype(jnp.bfloat16), "slab", 1).astype(jnp.float32)
    totals = totals[:span_x].at[:3].add(rim_planes)
    rim_rows = passed_along(totals[:, span_y:].astype(jnp.bfloat16), "pencil", 1).astype(
        jnp.float32
    )
    return totals[:, :span_y].at[:, :3].add(rim_rows)


def interpolate(grid_vals, cell_ids, stencil, blocks_run, block_len, slots):
    ghost_planes = passed_along(grid_vals[:3], "slab", -1)
    grid_vals = jnp.concatenate([grid_vals, ghost_planes], axis=0)
    ghost_rows = passed_along(grid_vals[:, :3], "pencil", -1)
    grid_vals = jnp.concatenate([grid_vals, ghost_rows], axis=1)
    channels = grid_vals.shape[3]
    flattened = grid_vals.reshape(-1, channels)

    def take_block(number, result):
        picked = (
            flattened[cell_ids.reshape(-1)].reshape(64, block_len, channels).astype(jnp.float32)
        )
        summed = jnp.sum(stencil[:, :, None] * picked, axis=0).astype(jnp.bfloat16)
        return summed

    return lax.fori_loop(0, blocks_run, take_block, jnp.zeros((slots, channels), jnp.bfloat16))


def forward_spectrum(density):
    section_one = transform(density, "xyzc,zk->xykc", False, True, False).astype(jnp.bfloat16)

    def along_y(block_vals):
        return transform(block_vals, "xyzc,yk->xkzc", False, False, False).astype(jnp.bfloat16)

    middle = along_y(lax.all_to_all(section_one, "pencil", split_axis=2, concat_axis=1, tiled=True))

    def along_x(block_vals):
        return transform(block_vals, "xyzc,xk->kyzc", False, False, False)

    return along_x(lax.all_to_all(middle, "slab", split_axis=1, concat_axis=0, tiled=True))


def back_to_cells(spectrum):
    section_one = transform(spectrum, "xyzc,xk->kyzc", True, False, False).astype(jnp.bfloat16)

    def along_y(block_vals):
        return transform(block_vals, "xyzc,yk->xkzc", True, False, False).astype(jnp.bfloat16)

    middle = along_y(lax.all_to_all(section_one, "slab", split_axis=0, concat_axis=1, tiled=True))

    def along_z(block_vals):
        return transform(block_vals, "xyzc,zk->xykc", True, False, True).astype(jnp.bfloat16)

    return along_z(lax.all_to_all(middle, "pencil", split_axis=1, concat_axis=2, tiled=True))


def per_device(charges, cotangent, base_cell, frac, counts, filter_weights):
    charges = charges.T
    cotangent = cotangent.T
    slab_index = lax.axis_index("slab")
    pencil_index = lax.axis_index("pencil")
    span_x = N // lax.axis_size("slab")
    span_y = N // lax.axis_size("pencil")
    slots = charges.shape[0]
    block_len = min(512, slots)
    live_count = counts[0]
    live = (jnp.arange(slots, dtype=jnp.int32) < live_count).astype(jnp.float32)
    cell_ids, stencil = stencil_local(
        base_cell, frac, live, slab_index * span_x, pencil_index * span_y, span_y
    )
    blocks_run = slots // block_len
    shells = filter_shells(slab_index * span_x, pencil_index * span_y, span_x, span_y)
    profile = jnp.dot(shells, filter_weights, precision=lax.Precision.HIGHEST).reshape(
        N, span_x, span_y, C
    )
    doubled = jnp.tile(profile, (1, 1, 1, 2))
    spectrum_q = forward_spectrum(spread(charges, cell_ids, stencil, span_x, span_y, blocks_run))
    potential = interpolate(
        back_to_cells(spectrum_q * doubled), cell_ids, stencil, blocks_run, block_len, slots
    )
    spectrum_g = forward_spectrum(spread(cotangent, cell_ids, stencil, span_x, span_y, blocks_run))
    correlation = (
        spectrum_g[..., :C] * spectrum_q[..., :C] + spectrum_g[..., C:] * spectrum_q[..., C:]
    )
    charge_grad = interpolate(
        back_to_cells(spectrum_g * doubled), cell_ids, stencil, blocks_run, block_len, slots
    )
    partial_grad = jnp.dot(
        shells.T, correlation.reshape(-1, C), precision=lax.Precision.HIGHEST
    ) / (N * N * N)
    filter_grad = lax.psum(partial_grad, ("slab", "pencil"))
    return (potential.T, charge_grad.T, filter_grad)


def solution(mesh):
    in_specs = (
        P(None, ("slab", "pencil")),
        P(None, ("slab", "pencil")),
        P(None, ("slab", "pencil")),
        P(None, ("slab", "pencil")),
        P(("slab", "pencil")),
        P(),
    )
    out_specs = (P(None, ("slab", "pencil")), P(None, ("slab", "pencil")), P())
    return jax.shard_map(
        per_device, mesh=mesh, in_specs=in_specs, out_specs=out_specs, check_vma=False
    )
```

profile of v0, /device:TPU:1, one launch (start us, length us, event | category | flops | bytes accessed | tf_op | source)
XLA Modules:
  0.0 876.0 jit_solution(3839491875228261354)
XLA Ops:
  6.2 12.0 %bitcast_multiply_fusion.1 = (f32[32768,64]{1,0:T(8,128)}, f32[32768,64]{1,0:T(8,128)}) fusion(f32[512,64]{1,0:T(8,128)S(1)} %copy.19, f32[32768]{0:T(1024)S(1)} %multiply_multiply_fusion, f32[512,64]{1,0:T(8,128)S(1)} %copy.28), kind=kLoop, calls=%fused_computation.9 | loop fusion | flops 4194304 | bytes 17170432 | tf_op jit(solution)/shard_map/while/body/eval_jaxpr/mul | solution.py:111
  18.2 174.7 %scatter_custom_fusion.1 = f32[3136,64]{1,0:T(8,128)S(1)} fusion(s32[32768]{0:T(1024)S(1)} %bitcast.346, f32[32768,64]{1,0:T(8,128)} %get-tuple-element.117, f32[]{:T(128)} %constant.266.clone.1), kind=kCustom, calls=%fused_computation.96 | custom fusion | flops 2097152 | bytes 803328 | tf_op jit(solution)/shard_map/while/body/eval_jaxpr/scatter-add | solution.py:112
  193.6 2.1 collective-permute-start.4
  195.8 174.7 %scatter_custom_fusion = f32[3136,64]{1,0:T(8,128)S(1)} fusion(s32[32768]{0:T(1024)S(1)} %bitcast.347, f32[32768,64]{1,0:T(8,128)} %get-tuple-element.116, f32[]{:T(128)} %constant.266.clone.1), kind=kCustom, calls=%fused_computation.98 | custom fusion | flops 2097152 | bytes 803328 | tf_op jit(solution)/shard_map/while/body/eval_jaxpr/scatter-add | solution.py:112
  371.2 1.8 collective-permute-start
  380.6 2.1 add_dynamic-update-slice_fusion
  383.7 2.8 collective-permute-start.5
  386.5 1.3 add_dynamic-update-slice_fusion.1
  393.4 9.9 %all-to-all-start.4 = ((bf16[4,4,64,128]{3,1,0,2:T(4,128)(2,1)}), bf16[4,4,64,128]{3,1,0,2:T(4,128)(2,1)S(1)}, u32[]{:S(2)}, u32[]{:S(2)}) async-start(bf16[4,4,64,128]{3,1,0,2:T(4,128)(2,1)} %copy.29), calls=%async_computation.4 | async-start | bytes 524288 | tf_op jit(solution)/shard_map/all_to_all | solution.py:150
  406.8 8.1 all-to-all-done.4
  414.9 3.4 all-to-all-start
  421.5 8.0 all-to-all-done
  432.6 1.4 fusion.17
  434.0 1.4 fusion.19
  437.2 6.0 all-to-all-start.5
  443.3 1.4 fusion.3
  444.7 1.4 fusion.5
  447.9 3.2 all-to-all-done.5
  451.1 3.9 all-to-all-start.1
  457.3 5.1 all-to-all-done.1
  464.4 1.4 fusion.23
  469.8 1.5 fusion.64
  474.7 4.4 all-to-all-start.2
  479.1 1.8 convolution_subtract_fusion
  482.7 3.8 all-to-all-done.2
  486.5 3.6 all-to-all-start.6
  495.8 1.6 all-to-all-done.6
  500.2 1.4 convolution_add_fusion.18
  501.6 1.4 convolution_add_fusion.16
  503.0 1.4 fusion.11
  504.4 1.4 fusion.13
  506.9 8.0 all-to-all-start.3
  515.0 1.4 convolution_add_fusion.4
  516.4 1.4 convolution_add_fusion.2
  520.0 6.7 all-to-all-done.3
  526.7 3.4 all-to-all-start.7
  530.2 1.6 fusion.161
  533.4 7.7 all-to-all-done.7
  541.9 1.4 convolution_add_fusion.14
  543.7 2.3 collective-permute-start.2
  547.7 2.7 collective-permute-done.2
  550.4 1.2 collective-permute-start.3
  551.6 2.9 collective-permute-done.6
  556.8 1.3 fusion.48
  558.1 76.5 %psum.7 = f32[32,64]{1,0:T(8,128)} all-reduce(f32[32,64]{1,0:T(8,128)S(1)} %fusion.48), channel_id=1, replica_groups=mesh['slab'=16,'pencil'=16] {'slab','pencil'}, use_global_device_ids=true, to_apply=%region_4.5 | all-reduce | flops 2048 | bytes 16384 | tf_op jit(solution)/shard_map/psum | solution.py:206
  635.7 114.9 %gather_fusion = bf16[32768,64]{1,0:T(8,128)(2,1)} fusion(bf16[3136,64]{1,0:T(8,128)(2,1)S(1)} %bitcast.273, s32[32768]{0:T(1024)S(1)} %broadcast_clamp_fusion), kind=kCustom, calls=%fused_computation | custom fusion | bytes 8519680 | tf_op jit(solution)/shard_map/while/body/eval_jaxpr/gather | solution.py:136
  751.8 114.9 %gather_fusion.1 = bf16[32768,64]{1,0:T(8,128)(2,1)} fusion(bf16[3136,64]{1,0:T(8,128)(2,1)S(1)} %bitcast.272, s32[32768]{0:T(1024)S(1)} %broadcast_clamp_fusion), kind=kCustom, calls=%fused_computation.1 | custom fusion | bytes 8519680 | tf_op jit(solution)/shard_map/while/body/eval_jaxpr/gather | solution.py:136
  866.7 7.5 fusion
  (173 shorter events, 69.3 us)
Async XLA Ops:
  0.6 376.4 %copy-start = (f32[32,64]{1,0:T(8,128)S(1)}, f32[32,64]{1,0:T(8,128)}, u32[]{:S(2)}) copy-start(f32[32,64]{1,0:T(8,128)} %param.19) | copy-start | bytes 24580
  1.4 0.9 copy-start.10
  2.3 15.9 %copy-start.11 = (f32[512]{0:T(512)}, f32[512]{0:T(512)S(1)}, u32[]{:S(2)}) copy-start(f32[512]{0:T(512)S(1)} %fusion.301) | copy-start | bytes 6148
  6.1 189.7 %copy-start.5 = (s32[32768,1]{0,1:T(1,128)}, s32[32768,1]{0,1:T(1,128)S(1)}, u32[]{:S(2)}) copy-start(s32[32768,1]{0,1:T(1,128)S(1)} %compare_select_fusion) | copy-start | bytes 393220
  193.6 186.9 %collective-permute-start.4 = (bf16[3,7,64,64]{3,2,1,0:T(8,128)(2,1)}, bf16[3,7,64,64]{3,2,1,0:T(8,128)(2,1)}, u32[]{:S(2)}, u32[]{:S(2)}) collective-permute-start(bf16[3,7,64,64]{3,2,1,0:T(8,128)(2,1)} %bitcast.66), channel_id=1, source_target_pairs={{0,16},{16,32},{32,48},{48,64},{64,80},{80,96},{96,112},{112,128},... | collective-permute-start | bytes 516104 | tf_op jit(solution)/shard_map/ppermute | solution.py:16
  371.2 15.2 %collective-permute-start = (bf16[3,7,64,64]{3,2,1,0:T(8,128)(2,1)}, bf16[3,7,64,64]{3,2,1,0:T(8,128)(2,1)}, u32[]{:S(2)}, u32[]{:S(2)}) collective-permute-start(bf16[3,7,64,64]{3,2,1,0:T(8,128)(2,1)} %bitcast.21), channel_id=1, source_target_pairs={{0,16},{16,32},{32,48},{48,64},{64,80},{80,96},{96,112},{112,128},... | collective-permute-start | bytes 516104 | tf_op jit(solution)/shard_map/ppermute | solution.py:16
  375.9 29.1 %copy-start.13 = (f32[32]{0:T(128)}, f32[32]{0:T(128)S(1)}, u32[]{:S(2)}) copy-start(f32[32]{0:T(128)S(1)} %iota_add_fusion) | copy-start | bytes 388
  377.0 28.7 %copy-start.6 = (f32[64,4,4]{0,2,1:T(4,128)}, f32[64,4,4]{0,2,1:T(4,128)S(1)}, u32[]{:S(2)}) copy-start(f32[64,4,4]{0,2,1:T(4,128)S(1)} %get-tuple-element.128) | copy-start | bytes 12292
  377.0 28.7 %copy-start.8 = (f32[64,4,4]{0,2,1:T(4,128)}, f32[64,4,4]{0,2,1:T(4,128)S(1)}, u32[]{:S(2)}) copy-start(f32[64,4,4]{0,2,1:T(4,128)S(1)} %get-tuple-element.129) | copy-start | bytes 12292
  383.7 6.1 collective-permute-start.5
  388.9 14.4 %collective-permute-start.1 = (bf16[4,3,64,64]{3,2,1,0:T(8,128)(2,1)S(1)}, bf16[4,3,64,64]{3,2,1,0:T(8,128)(2,1)}, u32[]{:S(2)}, u32[]{:S(2)}) collective-permute-start(bf16[4,3,64,64]{3,2,1,0:T(8,128)(2,1)S(1)} %slice.473), channel_id=1, source_target_pairs={{0,1},{1,2},{2,3},{3,4},{4,5},{5,6},{6,7},{7,8},{8,9},{9,10},{10,1... | collective-permute-start | bytes 294920 | tf_op jit(solution)/shard_map/ppermute | solution.py:16
  393.4 21.5 %all-to-all-start.4 = ((bf16[4,4,64,128]{3,1,0,2:T(4,128)(2,1)}), bf16[4,4,64,128]{3,1,0,2:T(4,128)(2,1)S(1)}, u32[]{:S(2)}, u32[]{:S(2)}) async-start(bf16[4,4,64,128]{3,1,0,2:T(4,128)(2,1)} %copy.29), calls=%async_computation.4 | async-start | bytes 524288 | tf_op jit(solution)/shard_map/all_to_all | solution.py:150
  414.9 14.6 %all-to-all-start = ((bf16[4,4,64,128]{3,1,0,2:T(4,128)(2,1)}), bf16[4,4,64,128]{3,1,0,2:T(4,128)(2,1)S(1)}, u32[]{:S(2)}, u32[]{:S(2)}) async-start(bf16[4,4,64,128]{3,1,0,2:T(4,128)(2,1)} %copy.20), calls=%async_computation | async-start | bytes 524288 | tf_op jit(solution)/shard_map/all_to_all | solution.py:150
  437.2 13.9 %all-to-all-start.5 = ((bf16[4,64,4,128]{3,2,0,1:T(4,128)(2,1)}), bf16[4,64,4,128]{3,2,0,1:T(4,128)(2,1)S(1)}, u32[]{:S(2)}, u32[]{:S(2)}) async-start(bf16[4,64,4,128]{3,2,0,1:T(4,128)(2,1)} %copy.31), calls=%async_computation.5 | async-start | bytes 524288 | tf_op jit(solution)/shard_map/all_to_all | solution.py:155
  451.1 11.3 %all-to-all-start.1 = ((bf16[4,64,4,128]{3,2,0,1:T(4,128)(2,1)}), bf16[4,64,4,128]{3,2,0,1:T(4,128)(2,1)S(1)}, u32[]{:S(2)}, u32[]{:S(2)}) async-start(bf16[4,64,4,128]{3,2,0,1:T(4,128)(2,1)} %copy.22), calls=%async_computation.1 | async-start | bytes 524288 | tf_op jit(solution)/shard_map/all_to_all | solution.py:155
  474.7 11.9 %all-to-all-start.2 = ((bf16[64,4,4,128]{3,2,1,0:T(4,128)(2,1)}), bf16[64,4,4,128]{3,2,1,0:T(4,128)(2,1)}, u32[]{:S(2)}, u32[]{:S(2)}) async-start(bf16[64,4,4,128]{3,2,1,0:T(4,128)(2,1)} %copy.24), calls=%async_computation.2 | async-start | bytes 524288 | tf_op jit(solution)/shard_map/all_to_all | solution.py:164
  486.5 10.9 %all-to-all-start.6 = ((bf16[64,4,4,128]{3,2,1,0:T(4,128)(2,1)}), bf16[64,4,4,128]{3,2,1,0:T(4,128)(2,1)S(1)}, u32[]{:S(2)}, u32[]{:S(2)}) async-start(bf16[64,4,4,128]{3,2,1,0:T(4,128)(2,1)} %copy.33), calls=%async_computation.6 | async-start | bytes 524288 | tf_op jit(solution)/shard_map/all_to_all | solution.py:164
  501.6 28.6 %copy-start.12 = (f32[512]{0:T(512)S(1)}, f32[512]{0:T(512)}, u32[]{:S(2)}) copy-start(f32[512]{0:T(512)} %copy-done.11) | copy-start | bytes 6148
  506.9 19.8 %all-to-all-start.3 = ((bf16[4,64,4,128]{3,2,0,1:T(4,128)(2,1)}), bf16[4,64,4,128]{3,2,0,1:T(4,128)(2,1)S(1)}, u32[]{:S(2)}, u32[]{:S(2)}) async-start(bf16[4,64,4,128]{3,2,0,1:T(4,128)(2,1)} %copy.26), calls=%async_computation.3 | async-start | bytes 524288 | tf_op jit(solution)/shard_map/all_to_all | solution.py:169
  518.5 38.3 %copy-start.7 = (f32[64,4,4]{0,2,1:T(4,128)S(1)}, f32[64,4,4]{0,2,1:T(4,128)}, u32[]{:S(2)}) copy-start(f32[64,4,4]{0,2,1:T(4,128)} %copy-done.6) | copy-start | bytes 12292
  518.5 38.3 %copy-start.9 = (f32[64,4,4]{0,2,1:T(4,128)S(1)}, f32[64,4,4]{0,2,1:T(4,128)}, u32[]{:S(2)}) copy-start(f32[64,4,4]{0,2,1:T(4,128)} %copy-done.8) | copy-start | bytes 12292
  526.7 14.4 %all-to-all-start.7 = ((bf16[4,64,4,128]{3,2,0,1:T(4,128)(2,1)}), bf16[4,64,4,128]{3,2,0,1:T(4,128)(2,1)S(1)}, u32[]{:S(2)}, u32[]{:S(2)}) async-start(bf16[4,64,4,128]{3,2,0,1:T(4,128)(2,1)} %copy.35), calls=%async_computation.7 | async-start | bytes 524288 | tf_op jit(solution)/shard_map/all_to_all | solution.py:169
  543.7 6.6 collective-permute-start.2
  546.8 7.8 collective-permute-start.6
  550.4 84.2 %collective-permute-start.3 = (bf16[7,3,64,64]{3,2,1,0:T(8,128)(2,1)S(1)}, bf16[7,3,64,64]{3,2,1,0:T(8,128)(2,1)}, u32[]{:S(2)}, u32[]{:S(2)}) collective-permute-start(bf16[7,3,64,64]{3,2,1,0:T(8,128)(2,1)S(1)} %pad_maximum_fusion.3), channel_id=1, source_target_pairs={{0,15},{1,0},{2,1},{3,2},{4,3},{5,4},{6,5},{7,6},{8,7},{9,8},{10,9... | collective-permute-start | bytes 516104 | tf_op jit(solution)/shard_map/ppermute | solution.py:16
  554.5 0.7 copy-start.2
  556.0 194.6 %collective-permute-start.7 = (bf16[7,3,64,64]{3,2,1,0:T(8,128)(2,1)}, bf16[7,3,64,64]{3,2,1,0:T(8,128)(2,1)}, u32[]{:S(2)}, u32[]{:S(2)}) collective-permute-start(bf16[7,3,64,64]{3,2,1,0:T(8,128)(2,1)} %pad_maximum_fusion.2), channel_id=1, source_target_pairs={{0,15},{1,0},{2,1},{3,2},{4,3},{5,4},{6,5},{7,6},{8,7},{9,8},{10,9... | collective-permute-start | bytes 516104 | tf_op jit(solution)/shard_map/ppermute | solution.py:16
  635.7 114.9 %copy-start.3 = (bf16[3,4,64,64]{3,2,1,0:T(8,128)(2,1)S(1)}, bf16[3,4,64,64]{3,2,1,0:T(8,128)(2,1)}, u32[]{:S(2)}) copy-start(bf16[3,4,64,64]{3,2,1,0:T(8,128)(2,1)} %copy-done.2) | copy-start | bytes 294916
  751.8 114.9 %copy-start.4 = (f32[64,512]{1,0:T(8,128)S(1)}, f32[64,512]{1,0:T(8,128)}, u32[]{:S(2)}) copy-start(f32[64,512]{1,0:T(8,128)} %fusion.161) | copy-start | bytes 393220
  866.7 9.0 %copy-start.1 = (f32[32,64]{1,0:T(8,128)S(1)}, f32[32,64]{1,0:T(8,128)}, u32[]{:S(2)}) copy-start(f32[32,64]{1,0:T(8,128)} %param.19) | copy-start | bytes 24580
where the time goes:
time: 884 us; the launch traced here: 876 us
  other arithmetic  386 us (44%)
  local copies, waits for them, and re-layouts  251 us (28%)
  blocking collectives  76.5 us (9%)
  starting transfers between devices  55.5 us (6%)
  matrix products  54.9 us (6%)
  waiting for transfers between devices  49.8 us (6%)
    scatter-add x2, other arithmetic, add_block(): return totals.at[cell_ids.reshape(-1)].add(products.reshape(-1, channels))  349 us
    gather x2, local copies, waits for them, and re-layouts, take_block(): flattened[cell_ids.reshape(-1)].reshape(64, block_len, channels)  230 us
    psum x1, blocking collectives, per_device(): filter_grad = lax.psum(partial_grad, ('slab', 'pencil'))  76.5 us
    dot_general x28, matrix products, contract(): jnp.einsum(pattern, operand, table_low, preferred_element_type=jnp.float32)  22.5 us
    dot_general x28, matrix products, contract(): jnp.einsum(pattern, operand, table_high, preferred_element_type=jnp.float32)  19.5 us
  transfers between devices with their start and end apart: 16, of which 10 were waited for; matrix products, arithmetic and copies ran while one was open for 39% of the time, Pallas kernels for 0%

commit v1 on v0

--- a/solution.py
+++ b/solution.py
@@ -203,7 +203,7 @@
     partial_grad = jnp.dot(
         shells.T, correlation.reshape(-1, C), precision=lax.Precision.HIGHEST
     ) / (N * N * N)
-    filter_grad = lax.psum(partial_grad, ("slab", "pencil"))
+    filter_grad = jnp.sum(lax.all_gather(partial_grad, ("slab", "pencil")), axis=0)
     return (potential.T, charge_grad.T, filter_grad)
 
 

time: 884 us -> 809 us (0.915)
  blocking collectives: 76.5 us -> 0 us
  matrix products: 54.9 us -> 40.7 us
  between operations: 2.63 us -> 16 us
  waiting for transfers between devices: 49.8 us -> 59.5 us
    psum x1 -> x0, blocking collectives: 76.5 us -> none  [per_device(): filter_grad = lax.psum(partial_grad, ('slab', 'pencil'))]
  transfers between devices with their start and end apart: 16 -> 17, of which waited for: 10 -> 10; matrix products, arithmetic and copies ran while one was open for 39% -> 57% of each run, Pallas kernels for 0% -> 0%
where the time goes in v1:
time: 809 us; the launch traced here: 801 us
  other arithmetic  384 us (47%)
  local copies, waits for them, and re-layouts  248 us (31%)
  waiting for transfers between devices  59.5 us (7%)
  starting transfers between devices  52.7 us (7%)
  matrix products  40.7 us (5%)
  between operations  16 us (2%)
    scatter-add x2, other arithmetic, add_block(): return totals.at[cell_ids.reshape(-1)].add(products.reshape(-1, channels))  349 us
    gather x2, local copies, waits for them, and re-layouts, take_block(): flattened[cell_ids.reshape(-1)].reshape(64, block_len, channels)  228 us
    all_to_all x2, waiting for transfers between devices, back_to_cells(): lax.all_to_all(middle, 'pencil', split_axis=1, concat_axis=2, tiled=True)  17.5 us
    all_to_all x2, waiting for transfers between devices, forward_spectrum(): lax.all_to_all(section_one, 'pencil', split_axis=2, concat_axis=1, tiled=...  17 us
  transfers between devices with their start and end apart: 17, of which 10 were waited for; matrix products, arithmetic and copies ran while one was open for 57% of the time, Pallas kernels for 0%

profile of v1, /device:TPU:1, one launch (start us, length us, event | category | flops | bytes accessed | tf_op | source)
XLA Modules:
  0.0 801.2 jit_solution(4918861347492805706)
XLA Ops:
  12.7 12.0 %bitcast_multiply_fusion.1 = (f32[32768,64]{1,0:T(8,128)}, f32[32768,64]{1,0:T(8,128)}) fusion(f32[512,64]{1,0:T(8,128)S(1)} %copy.19, f32[32768]{0:T(1024)S(1)} %multiply_multiply_fusion, f32[512,64]{1,0:T(8,128)S(1)} %copy.28), kind=kLoop, calls=%fused_computation.9 | loop fusion | flops 4194304 | bytes 17170432 | tf_op jit(solution)/shard_map/while/body/eval_jaxpr/mul | solution.py:111
  24.7 174.7 %scatter_custom_fusion.1 = f32[3136,64]{1,0:T(8,128)S(1)} fusion(s32[32768]{0:T(1024)S(1)} %bitcast.349, f32[32768,64]{1,0:T(8,128)} %get-tuple-element.117, f32[]{:T(128)} %constant.267.clone.1), kind=kCustom, calls=%fused_computation.96 | custom fusion | flops 2097152 | bytes 803328 | tf_op jit(solution)/shard_map/while/body/eval_jaxpr/scatter-add | solution.py:112
  200.1 2.1 collective-permute-start.4
  202.3 174.7 %scatter_custom_fusion = f32[3136,64]{1,0:T(8,128)S(1)} fusion(s32[32768]{0:T(1024)S(1)} %bitcast.350, f32[32768,64]{1,0:T(8,128)} %get-tuple-element.116, f32[]{:T(128)} %constant.267.clone.1), kind=kCustom, calls=%fused_computation.98 | custom fusion | flops 2097152 | bytes 803328 | tf_op jit(solution)/shard_map/while/body/eval_jaxpr/scatter-add | solution.py:112
  377.7 1.7 collective-permute-start
  383.2 1.1 fusion.74
  384.6 1.4 tile.35
  386.8 2.1 add_dynamic-update-slice_fusion
  390.0 2.8 collective-permute-start.5
  392.7 1.3 add_dynamic-update-slice_fusion.1
  394.0 1.1 slice.316
  395.2 1.1 collective-permute-start.1
  396.2 1.0 fusion.72
  399.8 9.8 %all-to-all-start.4 = ((bf16[4,4,64,128]{3,1,0,2:T(4,128)(2,1)}), bf16[4,4,64,128]{3,1,0,2:T(4,128)(2,1)S(1)}, u32[]{:S(2)}, u32[]{:S(2)}) async-start(bf16[4,4,64,128]{3,1,0,2:T(4,128)(2,1)} %copy.29), calls=%async_computation.4 | async-start | bytes 524288 | tf_op jit(solution)/shard_map/all_to_all | solution.py:150
  412.1 9.0 %all-to-all-done.4 = bf16[4,4,64,128]{3,1,0,2:T(4,128)(2,1)S(1)} async-done(((bf16[4,4,64,128]{3,1,0,2:T(4,128)(2,1)}), bf16[4,4,64,128]{3,1,0,2:T(4,128)(2,1)S(1)}, u32[]{:S(2)}, u32[]{:S(2)}) %all-to-all-start.4) | async-done | bytes 262176 | tf_op jit(solution)/shard_map/all_to_all | solution.py:150
  421.2 3.4 all-to-all-start
  424.7 1.2 fusion.115
  426.2 1.2 fusion.118
  427.8 8.0 all-to-all-done
  436.6 1.1 fusion.154
  438.1 1.4 fusion.17
  439.5 1.4 fusion.19
  442.7 6.0 all-to-all-start.5
  449.1 1.4 fusion.5
  452.3 4.3 all-to-all-done.5
  456.6 3.9 all-to-all-start.1
  462.1 5.8 all-to-all-done.1
  472.4 1.9 fusion.48
  474.2 1.4 maximum_multiply_fusion
  481.2 3.8 all-to-all-start.2
  487.6 4.8 all-to-all-done.2
  492.4 3.6 all-to-all-start.6
  496.1 1.2 fusion.127
  497.6 1.1 fusion.130
  499.2 4.2 all-to-all-done.6
  504.5 1.4 convolution_add_fusion.18
  505.9 1.4 convolution_add_fusion.16
  509.2 8.1 %all-to-all-start.3 = ((bf16[4,64,4,128]{3,2,0,1:T(4,128)(2,1)}), bf16[4,64,4,128]{3,2,0,1:T(4,128)(2,1)S(1)}, u32[]{:S(2)}, u32[]{:S(2)}) async-start(bf16[4,64,4,128]{3,2,0,1:T(4,128)(2,1)} %copy.26), calls=%async_computation.3 | async-start | bytes 524288 | tf_op jit(solution)/shard_map/all_to_all | solution.py:169
  520.2 8.8 %all-to-all-done.3 = bf16[4,64,4,128]{3,2,0,1:T(4,128)(2,1)S(1)} async-done(((bf16[4,64,4,128]{3,2,0,1:T(4,128)(2,1)}), bf16[4,64,4,128]{3,2,0,1:T(4,128)(2,1)S(1)}, u32[]{:S(2)}, u32[]{:S(2)}) %all-to-all-start.3) | async-done | bytes 262176 | tf_op jit(solution)/shard_map/all_to_all | solution.py:169
  529.0 3.4 all-to-all-start.7
  534.0 1.1 collective-permute-start.2
  535.2 8.7 %all-to-all-done.7 = bf16[4,64,4,128]{3,2,0,1:T(4,128)(2,1)S(1)} async-done(((bf16[4,64,4,128]{3,2,0,1:T(4,128)(2,1)}), bf16[4,64,4,128]{3,2,0,1:T(4,128)(2,1)S(1)}, u32[]{:S(2)}, u32[]{:S(2)}) %all-to-all-start.7) | async-done | bytes 262176 | tf_op jit(solution)/shard_map/all_to_all | solution.py:169
  545.5 1.1 collective-permute-start.6
  546.8 5.5 collective-permute-done.6
  553.6 114.1 %gather_fusion = bf16[32768,64]{1,0:T(8,128)(2,1)} fusion(bf16[3136,64]{1,0:T(8,128)(2,1)S(1)} %bitcast.274, s32[32768]{0:T(1024)S(1)} %broadcast_clamp_fusion), kind=kCustom, calls=%fused_computation | custom fusion | bytes 8519680 | tf_op jit(solution)/shard_map/while/body/eval_jaxpr/gather | solution.py:136
  667.9 114.1 %gather_fusion.1 = bf16[32768,64]{1,0:T(8,128)(2,1)} fusion(bf16[3136,64]{1,0:T(8,128)(2,1)S(1)} %bitcast.273, s32[32768]{0:T(1024)S(1)} %broadcast_clamp_fusion), kind=kCustom, calls=%fused_computation.1 | custom fusion | bytes 8519680 | tf_op jit(solution)/shard_map/while/body/eval_jaxpr/gather | solution.py:136
  782.0 7.5 fusion
  791.0 3.1 reduce_sum.31
  (168 shorter events, 50.1 us)
Async XLA Ops:
  7.2 376.0 %copy-start = (f32[32,64]{1,0:T(8,128)S(1)}, f32[32,64]{1,0:T(8,128)}, u32[]{:S(2)}) copy-start(f32[32,64]{1,0:T(8,128)} %param.19) | copy-start | bytes 24580
  8.0 0.9 copy-start.6
  8.8 15.9 %copy-start.7 = (f32[512]{0:T(512)}, f32[512]{0:T(512)S(1)}, u32[]{:S(2)}) copy-start(f32[512]{0:T(512)S(1)} %fusion.301) | copy-start | bytes 6148
  200.1 186.7 %collective-permute-start.4 = (bf16[3,7,64,64]{3,2,1,0:T(8,128)(2,1)}, bf16[3,7,64,64]{3,2,1,0:T(8,128)(2,1)}, u32[]{:S(2)}, u32[]{:S(2)}) collective-permute-start(bf16[3,7,64,64]{3,2,1,0:T(8,128)(2,1)} %bitcast.66), channel_id=1, source_target_pairs={{0,16},{16,32},{32,48},{48,64},{64,80},{80,96},{96,112},{112,128},... | collective-permute-start | bytes 516104 | tf_op jit(solution)/shard_map/ppermute | solution.py:16
  377.7 15.0 %collective-permute-start = (bf16[3,7,64,64]{3,2,1,0:T(8,128)(2,1)}, bf16[3,7,64,64]{3,2,1,0:T(8,128)(2,1)}, u32[]{:S(2)}, u32[]{:S(2)}) collective-permute-start(bf16[3,7,64,64]{3,2,1,0:T(8,128)(2,1)} %bitcast.21), channel_id=1, source_target_pairs={{0,16},{16,32},{32,48},{48,64},{64,80},{80,96},{96,112},{112,128},... | collective-permute-start | bytes 516104 | tf_op jit(solution)/shard_map/ppermute | solution.py:16
  382.4 0.6 copy-start.9
  382.5 0.6 copy-start.2
  382.6 0.6 copy-start.4
  390.0 6.3 collective-permute-start.5
  395.2 14.4 %collective-permute-start.1 = (bf16[4,3,64,64]{3,2,1,0:T(8,128)(2,1)S(1)}, bf16[4,3,64,64]{3,2,1,0:T(8,128)(2,1)S(1)}, u32[]{:S(2)}, u32[]{:S(2)}) collective-permute-start(bf16[4,3,64,64]{3,2,1,0:T(8,128)(2,1)S(1)} %slice.473), channel_id=1, source_target_pairs={{0,1},{1,2},{2,3},{3,4},{4,5},{5,6},{6,7},{7,8},{8,9},{9,10},{10,1... | collective-permute-start | bytes 294920 | tf_op jit(solution)/shard_map/ppermute | solution.py:16
  399.8 21.4 %all-to-all-start.4 = ((bf16[4,4,64,128]{3,1,0,2:T(4,128)(2,1)}), bf16[4,4,64,128]{3,1,0,2:T(4,128)(2,1)S(1)}, u32[]{:S(2)}, u32[]{:S(2)}) async-start(bf16[4,4,64,128]{3,1,0,2:T(4,128)(2,1)} %copy.29), calls=%async_computation.4 | async-start | bytes 524288 | tf_op jit(solution)/shard_map/all_to_all | solution.py:150
  421.2 14.6 %all-to-all-start = ((bf16[4,4,64,128]{3,1,0,2:T(4,128)(2,1)}), bf16[4,4,64,128]{3,1,0,2:T(4,128)(2,1)S(1)}, u32[]{:S(2)}, u32[]{:S(2)}) async-start(bf16[4,4,64,128]{3,1,0,2:T(4,128)(2,1)} %copy.20), calls=%async_computation | async-start | bytes 524288 | tf_op jit(solution)/shard_map/all_to_all | solution.py:150
  442.7 13.9 %all-to-all-start.5 = ((bf16[4,64,4,128]{3,2,0,1:T(4,128)(2,1)}), bf16[4,64,4,128]{3,2,0,1:T(4,128)(2,1)S(1)}, u32[]{:S(2)}, u32[]{:S(2)}) async-start(bf16[4,64,4,128]{3,2,0,1:T(4,128)(2,1)} %copy.31), calls=%async_computation.5 | async-start | bytes 524288 | tf_op jit(solution)/shard_map/all_to_all | solution.py:155
  456.6 11.3 %all-to-all-start.1 = ((bf16[4,64,4,128]{3,2,0,1:T(4,128)(2,1)}), bf16[4,64,4,128]{3,2,0,1:T(4,128)(2,1)S(1)}, u32[]{:S(2)}, u32[]{:S(2)}) async-start(bf16[4,64,4,128]{3,2,0,1:T(4,128)(2,1)} %copy.22), calls=%async_computation.1 | async-start | bytes 524288 | tf_op jit(solution)/shard_map/all_to_all | solution.py:155
  460.5 330.5 %all-gather.3.cloned.1.call-start = ((), (), s32[]{:S(2)}) async-start(), calls=%async_computation.8 | async-start | bytes 4210688 | tf_op jit(solution)/shard_map/all_gather | solution.py:206
  461.7 10.7 %copy-start.3 = (f32[64,4,4]{0,2,1:T(4,128)S(1)}, f32[64,4,4]{0,2,1:T(4,128)}, u32[]{:S(2)}) copy-start(f32[64,4,4]{0,2,1:T(4,128)} %copy-done.2) | copy-start | bytes 12292
  461.7 10.7 %copy-start.5 = (f32[64,4,4]{0,2,1:T(4,128)S(1)}, f32[64,4,4]{0,2,1:T(4,128)}, u32[]{:S(2)}) copy-start(f32[64,4,4]{0,2,1:T(4,128)} %copy-done.4) | copy-start | bytes 12292
  481.2 11.2 %all-to-all-start.2 = ((bf16[64,4,4,128]{3,2,1,0:T(4,128)(2,1)}), bf16[64,4,4,128]{3,2,1,0:T(4,128)(2,1)S(1)}, u32[]{:S(2)}, u32[]{:S(2)}) async-start(bf16[64,4,4,128]{3,2,1,0:T(4,128)(2,1)} %copy.24), calls=%async_computation.2 | async-start | bytes 524288 | tf_op jit(solution)/shard_map/all_to_all | solution.py:164
  492.4 11.0 %all-to-all-start.6 = ((bf16[64,4,4,128]{3,2,1,0:T(4,128)(2,1)}), bf16[64,4,4,128]{3,2,1,0:T(4,128)(2,1)S(1)}, u32[]{:S(2)}, u32[]{:S(2)}) async-start(bf16[64,4,4,128]{3,2,1,0:T(4,128)(2,1)} %copy.33), calls=%async_computation.6 | async-start | bytes 524288 | tf_op jit(solution)/shard_map/all_to_all | solution.py:164
  509.2 19.9 %all-to-all-start.3 = ((bf16[4,64,4,128]{3,2,0,1:T(4,128)(2,1)}), bf16[4,64,4,128]{3,2,0,1:T(4,128)(2,1)S(1)}, u32[]{:S(2)}, u32[]{:S(2)}) async-start(bf16[4,64,4,128]{3,2,0,1:T(4,128)(2,1)} %copy.26), calls=%async_computation.3 | async-start | bytes 524288 | tf_op jit(solution)/shard_map/all_to_all | solution.py:169
  518.7 34.2 %copy-start.8 = (f32[512]{0:T(512)S(1)}, f32[512]{0:T(512)}, u32[]{:S(2)}) copy-start(f32[512]{0:T(512)} %copy-done.7) | copy-start | bytes 6148
  529.0 14.9 %all-to-all-start.7 = ((bf16[4,64,4,128]{3,2,0,1:T(4,128)(2,1)}), bf16[4,64,4,128]{3,2,0,1:T(4,128)(2,1)S(1)}, u32[]{:S(2)}, u32[]{:S(2)}) async-start(bf16[4,64,4,128]{3,2,0,1:T(4,128)(2,1)} %copy.35), calls=%async_computation.7 | async-start | bytes 524288 | tf_op jit(solution)/shard_map/all_to_all | solution.py:169
  534.0 12.5 %collective-permute-start.2 = (bf16[3,4,64,64]{3,2,1,0:T(8,128)(2,1)S(1)}, bf16[3,4,64,64]{3,2,1,0:T(8,128)(2,1)S(1)}, u32[]{:S(2)}, u32[]{:S(2)}) collective-permute-start(bf16[3,4,64,64]{3,2,1,0:T(8,128)(2,1)S(1)} %slice.312), channel_id=1, source_target_pairs={{0,240},{16,0},{32,16},{48,32},{64,48},{80,64},{96,80},{112,96},{1... | collective-permute-start | bytes 294920 | tf_op jit(solution)/shard_map/ppermute | solution.py:16
  545.5 6.8 collective-permute-start.6
  546.7 6.8 collective-permute-start.3
  552.3 115.4 %collective-permute-start.7 = (bf16[7,3,64,64]{3,2,1,0:T(8,128)(2,1)S(1)}, bf16[7,3,64,64]{3,2,1,0:T(8,128)(2,1)S(1)}, u32[]{:S(2)}, u32[]{:S(2)}) collective-permute-start(bf16[7,3,64,64]{3,2,1,0:T(8,128)(2,1)S(1)} %pad_maximum_fusion.2), channel_id=1, source_target_pairs={{0,15},{1,0},{2,1},{3,2},{4,3},{5,4},{6,5},{7,6},{8,7},{9,8},{10,9... | collective-permute-start | bytes 516104 | tf_op jit(solution)/shard_map/ppermute | solution.py:16
  782.0 12.1 %copy-start.1 = (f32[32,64]{1,0:T(8,128)S(1)}, f32[32,64]{1,0:T(8,128)}, u32[]{:S(2)}) copy-start(f32[32,64]{1,0:T(8,128)} %param.19) | copy-start | bytes 24580
Sparse Core Ops, SparseCore 0:
  478.7 111.7 all-gather.2
